TPU v7x, 512 devices: a whole 4x8x8 slice. The times are simulated.
512 devices in a mesh: seq: 64 (over x, y, core), dp: 8 (over z).
Axes of the slice: x: 4, y: 8, z: 8, core: 2. Of those that a mesh axis runs over, the one named last changes fastest.
Arguments:
- query_proj: bfloat16 [163840, 1024], P(('dp', 'seq')), parts along dimension 0, may hold values from -8 to 8
- key_proj: bfloat16 [163840, 1024], P(('dp', 'seq')), parts along dimension 0, may hold values from -8 to 8
- value_proj: bfloat16 [163840, 1024], P(('dp', 'seq')), parts along dimension 0, may hold values from -6 to 6
- residual_in: bfloat16 [163840, 1024], P(('dp', 'seq')), parts along dimension 0, may hold values from -6 to 6
- utter_lengths: int32 [512], P('dp'), parts along dimension 0, may hold values from 1 to 640, 20480 in all
- depth_kernel: float32 [31, 1024], replicated, may hold values from -1 to 1
- norm_gain: float32 [1024], replicated, may hold values from 0.5 to 1.5
- norm_shift: float32 [1024], replicated, may hold values from -3 to 3
Outputs:
- block_out: bfloat16 [163840, 1024], P(('dp', 'seq')), parts along dimension 0
There are 8 independent parts, one for each index of `dp`. A program takes and returns all parts, laid end to end along the dimension named above; an argument that names none is the same for every part. Nothing has to cross between parts.
Inputs may be any that keep to these rules, and one draw needn't show every extreme that they name: `utter_lengths`: the lengths sum to 20480; the largest is exactly 640.
All inputs are finite; a program needn't handle non-finite values.
Results may differ from a plain program's by a relative error of at most 0.005.
Values may be sent and summed in bfloat16 or wider, within the bound.
A program may use at most 64 MiB of HBM per device.

v0:
```python
import functools

import jax
import jax.numpy as jnp
from jax import lax
from jax.experimental import pallas as pl
from jax.experimental.pallas import tpu as pltpu
from jax.sharding import PartitionSpec as P

MESH = pl.DeviceIdType.MESH
HALO = 16
TILES = 2
CONV_ROWS = 64
NORM_ROWS = 32
WINDOW = 1536
APART = -4096.0


def block_kernel(
    n,
    lens_hbm,
    taps_hbm,
    gain_hbm,
    shift_hbm,
    q_hbm,
    k_hbm,
    v_hbm,
    r_hbm,
    out_ref,
    lens_ref,
    taps_ref,
    gain_ref,
    shift_ref,
    qb,
    rb,
    kv,
    pb,
    lens_pad,
    kf,
    qf,
    after,
    before,
    mx,
    cv,
    small_sem,
    local_sem,
    halo_send,
    halo_recv,
    send_sem,
    recv_sem,
):
    rows, width = q_hbm.shape
    kb, vb = kv.at[0], kv.at[1]
    n_chunks = width // 128
    span = 5 * rows
    q_rows = rows + 2 * HALO
    me = lax.axis_index("seq")
    par = me % 2
    partner = me + 1 - 2 * par
    up = (me + 2) % n
    down = (me + n - 2) % n
    cross = (me + n - 1 + 2 * par) % n

    small = [
        pltpu.make_async_copy(src, dst, small_sem.at[i])
        for i, (src, dst) in enumerate(
            (
                (lens_hbm, lens_ref),
                (taps_hbm, taps_ref),
                (gain_hbm, gain_ref),
                (shift_hbm, shift_ref),
            )
        )
    ]
    for copy in small:
        copy.start()
    own = [
        pltpu.make_async_copy(k_hbm, kb.at[pl.ds(2 * rows, rows)], local_sem.at[0]),
        pltpu.make_async_copy(v_hbm, vb.at[pl.ds(2 * rows, rows)], local_sem.at[1]),
        pltpu.make_async_copy(q_hbm, qb.at[pl.ds(HALO, rows)], local_sem.at[2]),
        pltpu.make_async_copy(r_hbm, rb.at[pl.ds(HALO, rows)], local_sem.at[3]),
    ]
    for copy in own:
        copy.start()

    barrier = pltpu.get_barrier_semaphore()
    for other in (partner, up, down, cross):
        pl.semaphore_signal(barrier, inc=1, device_id={"seq": other}, device_id_type=MESH)
    pl.semaphore_wait(barrier, 4)

    def remote(src, dst, ssem, rsem, other):
        return pltpu.make_async_remote_copy(
            src_ref=src,
            dst_ref=dst,
            send_sem=ssem,
            recv_sem=rsem,
            device_id={"seq": other},
            device_id_type=MESH,
        )

    last = rows - HALO
    halos = []
    for side, other, src_row, dst_row in (
        (0, partner, last * (1 - par), (rows + HALO) * par),
        (1, cross, last * par, (rows + HALO) * (1 - par)),
    ):
        for which, src, dst in ((0, q_hbm, qb), (1, r_hbm, rb)):
            halos.append(
                remote(
                    src.at[pl.ds(pl.multiple_of(src_row, HALO), HALO)],
                    dst.at[pl.ds(pl.multiple_of(dst_row, HALO), HALO)],
                    halo_send.at[side, which],
                    halo_recv.at[side, which],
                    other,
                )
            )

    def columns(c):
        return pl.ds(pl.multiple_of(c * 128, 128), 128)

    def place(row):
        return pl.ds(pl.multiple_of(row, 32), rows)

    def send(c, kind, which):
        cols = columns(c)
        dst = kv.at[which]
        src = None if kind == 3 or not isinstance(which, int) else (k_hbm, v_hbm)[which]
        src = kv.at[which, pl.ds(2 * rows, rows)] if src is None else src
        src = src.at[:, cols]
        if kind == 0:
            args = src, dst.at[pl.ds(0, rows), cols], up
        elif kind == 1:
            args = src, dst.at[pl.ds(4 * rows, rows), cols], down
        elif kind == 2:
            args = src, dst.at[place(rows + 2 * rows * par), cols], partner
        else:
            args = (
                dst.at[place(4 * rows * (1 - par)), cols],
                dst.at[place(3 * rows - 2 * rows * par), cols],
                partner,
            )
        return remote(
            args[0],
            args[1],
            send_sem.at[kind, c, which],
            recv_sem.at[kind, c, which],
            args[2],
        )

    for copy in halos:
        copy.start()

    for which in (0, 1):

        def start_chunk(c, carry, which=which):
            for kind in (0, 1, 2):
                send(c, kind, which).start()
            return carry

        lax.fori_loop(0, n_chunks, start_chunk, 0)

    for copy in small:
        copy.wait()
    lens_pad[...] = jnp.zeros(lens_pad.shape, jnp.float32)
    lens_pad[:, pl.ds(0, lens_ref.shape[1])] = lens_ref[...].astype(jnp.float32)
    lens = lens_pad[...]
    low = lax.broadcasted_iota(jnp.int32, (128, 128), 0)
    lane = lax.broadcasted_iota(jnp.int32, (128, 128), 1)
    wide = jnp.broadcast_to(lens, (128, 128))
    tall = jnp.sum(jnp.where(low == lane, wide, 0.0), axis=1, keepdims=True)
    ends = jnp.sum(jnp.where(low <= lane, tall, 0.0), axis=0, keepdims=True)
    starts = ends - lens

    def member(first, count):
        pos = first + lax.broadcasted_iota(jnp.int32, (count, 128), 0)
        pos = pos.astype(jnp.float32)
        return pos, (pos >= starts) & (pos < ends)

    base = me * rows
    for part in range(5):
        _, inside = member(base + (part - 2) * rows, rows)
        kf[pl.ds(part * rows, rows), :] = jnp.where(inside, 0.0, APART).astype(jnp.bfloat16)
    _, inside = member(base - HALO, q_rows)
    qf[...] = jnp.where(inside, 1.0, 0.0).astype(jnp.bfloat16)
    pos, inside = member(base, rows)
    first = jnp.sum(jnp.where(inside, starts, 0.0), axis=1, keepdims=True)
    final = jnp.sum(jnp.where(inside, ends, 0.0), axis=1, keepdims=True)
    before[...] = pos - first
    after[...] = final - 1.0 - pos

    for copy in own:
        copy.wait()
    for copy in halos:
        copy.wait_recv()

    tile = q_rows // TILES
    window = WINDOW
    even = lax.broadcasted_iota(jnp.int32, (tile, 128), 1) < 64
    is_even = (lax.broadcasted_iota(jnp.int32, (1, 128), 1) < 64).astype(jnp.float32)
    lo = is_even.astype(jnp.bfloat16)
    hi = (1.0 - is_even).astype(jnp.bfloat16)
    ones = jnp.ones((window, 128), jnp.bfloat16)

    mx[:, columns(0)] = jnp.zeros((q_rows, 128), jnp.float32)
    half = taps_ref.shape[0] // 2

    def weigh(c):
        cols = columns(c)
        for t in range(TILES):
            mine = pl.ds(t * tile, tile)
            keys = pl.ds(t * (span - window), window)
            qt = qb[mine, cols] * jnp.bfloat16(0.125)
            feat = qf[mine, :]
            q2 = jnp.concatenate(
                [
                    jnp.concatenate([qt * lo, feat], axis=1),
                    jnp.concatenate([qt * hi, feat], axis=1),
                ],
                axis=0,
            )
            kk = jnp.concatenate([kb[keys, cols], kf[keys, :]], axis=1)
            s = lax.dot_general(
                q2, kk, (((1,), (1,)), ((), ())), preferred_element_type=jnp.float32
            )
            m = jnp.max(s, axis=1, keepdims=True)
            pb[c * TILES + t] = jnp.exp(s - m).astype(jnp.bfloat16)

    def convolve(c):
        cols = columns(c)
        for r in range(0, rows, CONV_ROWS):
            some = pl.ds(r, CONV_ROWS)
            room_before = before[some, :]
            room_after = after[some, :]
            acc = jnp.zeros((CONV_ROWS, 128), jnp.float32)
            for j in range(2 * half + 1):
                by = j - half
                x = mx[pl.ds(r + HALO + by, CONV_ROWS), cols]
                if by < 0:
                    x = jnp.where(room_before >= float(-by), x, 0.0)
                elif by > 0:
                    x = jnp.where(room_after >= float(by), x, 0.0)
                acc = acc + x * taps_ref[pl.ds(j, 1), cols]
            cv[some, cols] = acc

    def mix(c):
        cols = columns(c)
        for t in range(TILES):
            mine = pl.ds(t * tile, tile)
            keys = pl.ds(t * (span - window), window)
            vv = jnp.concatenate([vb[keys, cols], ones], axis=1)
            o = jnp.dot(pb[c * TILES + t], vv, preferred_element_type=jnp.float32)
            num = jnp.where(even, o[:tile, :128], o[tile:, :128])
            den = jnp.where(even, o[:tile, 128:], o[tile:, 128:])
            mixed = rb[mine, cols].astype(jnp.float32) + num / den
            mx[mine, cols] = mixed.astype(jnp.bfloat16).astype(jnp.float32)

    def step(i, carry):
        @pl.when(i < 2 * n_chunks)
        def _():
            which, c = i // n_chunks, i % n_chunks
            for kind in (0, 1):
                send(c, kind, which).wait_recv()
            send(c, 3, which).start()

        @pl.when((i >= 1) & (i <= n_chunks))
        def _():
            for kind in (2, 3):
                send(i - 1, kind, 0).wait_recv()
            weigh(i - 1)

        @pl.when(i > n_chunks)
        def _():
            c = i - 1 - n_chunks
            for kind in (2, 3):
                send(c, kind, 1).wait_recv()
            convolve(lax.max(c - 1, 0))
            mix(c)

        return carry

    lax.fori_loop(0, 2 * n_chunks + 1, step, 0)
    convolve(n_chunks - 1)

    for r in range(0, rows, NORM_ROWS):
        some = pl.ds(r, NORM_ROWS)
        x = cv[some, :]
        mean = jnp.sum(x, axis=1, keepdims=True) * (1.0 / width)
        x = x - mean
        var = jnp.sum(x * x, axis=1, keepdims=True) * (1.0 / width)
        normed = x * lax.rsqrt(var + 1e-05) * gain_ref[...] + shift_ref[...]
        gated = 0.5 * normed
        gated = gated + gated * jnp.tanh(gated)
        result = mx[pl.ds(r + HALO, NORM_ROWS), :] + gated
        out_ref[some, :] = result.astype(out_ref.dtype)

    for copy in halos:
        copy.wait_send()

    def finish(c, carry):
        for kind in range(4):
            for which in (0, 1):
                send(c, kind, which).wait_send()
        return carry

    lax.fori_loop(0, n_chunks, finish, 0)


def local(
    query_proj,
    key_proj,
    value_proj,
    residual_in,
    utter_lengths,
    depth_kernel,
    norm_gain,
    norm_shift,
):
    rows, width = query_proj.shape
    n = lax.axis_size("seq")
    n_chunks = width // 128
    q_rows, span = rows + 2 * HALO, 5 * rows
    vmem = pl.BlockSpec(memory_space=pltpu.VMEM)
    hbm = pl.BlockSpec(memory_space=pltpu.HBM)
    bf16, f32 = jnp.bfloat16, jnp.float32
    return pl.pallas_call(
        functools.partial(block_kernel, n),
        out_shape=jax.ShapeDtypeStruct((rows, width), bf16),
        in_specs=[hbm] * 8,
        out_specs=vmem,
        scratch_shapes=[
            pltpu.VMEM((1, utter_lengths.shape[0]), jnp.int32),
            pltpu.VMEM(depth_kernel.shape, f32),
            pltpu.VMEM((1, width), f32),
            pltpu.VMEM((1, width), f32),
            pltpu.VMEM((q_rows, width), bf16),
            pltpu.VMEM((q_rows, width), bf16),
            pltpu.VMEM((2, span, width), bf16),
            pltpu.VMEM((TILES * n_chunks, 2 * q_rows // TILES, WINDOW), bf16),
            pltpu.VMEM((1, 128), f32),
            pltpu.VMEM((span, 128), bf16),
            pltpu.VMEM((q_rows, 128), bf16),
            pltpu.VMEM((rows, 128), f32),
            pltpu.VMEM((rows, 128), f32),
            pltpu.VMEM((q_rows, width), f32),
            pltpu.VMEM((rows, width), f32),
            pltpu.SemaphoreType.DMA((4,)),
            pltpu.SemaphoreType.DMA((4,)),
            pltpu.SemaphoreType.DMA((2, 2)),
            pltpu.SemaphoreType.DMA((2, 2)),
            pltpu.SemaphoreType.DMA((4, n_chunks, 2)),
            pltpu.SemaphoreType.DMA((4, n_chunks, 2)),
        ],
        compiler_params=pltpu.CompilerParams(
            collective_id=0, has_side_effects=True, vmem_limit_bytes=44 << 20
        ),
        name="conformer_block",
    )(
        *(
            pltpu.with_memory_space_constraint(array, pltpu.HBM)
            for array in (
                utter_lengths.reshape(1, -1),
                depth_kernel,
                norm_gain.reshape(1, -1),
                norm_shift.reshape(1, -1),
                query_proj,
                key_proj,
                value_proj,
                residual_in,
            )
        )
    )


def solution(mesh):
    return jax.shard_map(
        local,
        mesh=mesh,
        in_specs=(
            P(("dp", "seq"), None),
            P(("dp", "seq"), None),
            P(("dp", "seq"), None),
            P(("dp", "seq"), None),
            P("dp"),
            P(),
            P(),
            P(),
        ),
        out_specs=P(("dp", "seq"), None),
        check_vma=False,
    )
```

profile of v0, /device:TPU:1, one launch (start us, length us, event | category | flops | bytes accessed | tf_op | source)
XLA Modules:
  0.0 49.5 jit_solution(9851583357321853263)
XLA Ops:
  0.0 48.6 %conformer_block.1 = bf16[320,1024]{1,0:T(8,128)(2,1)S(1)} custom-call(s32[1,64]{1,0:T(1,128)} %bitcast.5, f32[31,1024]{1,0:T(8,128)} %taps_hbm.1, f32[1,1024]{1,0:T(1,128)} %bitcast.3, f32[1,1024]{1,0:T(1,128)} %bitcast.4, bf16[320,1024]{1,0:T(8,128)(2,1)} %q_hbm.1, bf16[320,1024]{1,0:T(8,128)(2,1)} %k_hbm.1, bf16[320,1024]{1,0:T(8,128)(2,1)} %v_hbm.1, ...), custom_call_target="tpu_custom_call" | custom-call | tf_op jit(solution)/shard_map/conformer_block/pallas_call | solution.py:325
  48.6 0.8 %copy.10 = bf16[320,1024]{1,0:T(8,128)(2,1)} copy(bf16[320,1024]{1,0:T(8,128)(2,1)S(1)} %conformer_block.1) | data formatting | bytes 1310720
where the time goes:
time: 49.6 us; the launch traced here: 49.5 us
  Pallas kernels  48.6 us (98%)
  local copies, waits for them, and re-layouts  0.84 us (2%)
    pallas_call x1, Pallas kernels, local(): pl.pallas_call(functools.partial(block_kernel, n), out_shape=jax.ShapeDty...  48.6 us

commit v1 on v0

--- a/solution.py
+++ b/solution.py
@@ -31,6 +31,7 @@
     taps_ref,
     gain_ref,
     shift_ref,
+    passing,
     qb,
     rb,
     kv,
@@ -40,7 +41,9 @@
     qf,
     after,
     before,
-    mx,
+    mxs,
+    cvs,
+    mb,
     cv,
     small_sem,
     local_sem,
@@ -57,9 +60,8 @@
     me = lax.axis_index("seq")
     par = me % 2
     partner = me + 1 - 2 * par
-    up = (me + 2) % n
-    down = (me + n - 2) % n
-    cross = (me + n - 1 + 2 * par) % n
+    near = (me + n - 2 + 4 * par) % n
+    far = (me + n + 2 - 4 * par) % n
 
     small = [
         pltpu.make_async_copy(src, dst, small_sem.at[i])
@@ -84,9 +86,9 @@
         copy.start()
 
     barrier = pltpu.get_barrier_semaphore()
-    for other in (partner, up, down, cross):
+    for other in (partner, near, far):
         pl.semaphore_signal(barrier, inc=1, device_id={"seq": other}, device_id_type=MESH)
-    pl.semaphore_wait(barrier, 4)
+    pl.semaphore_wait(barrier, 3)
 
     def remote(src, dst, ssem, rsem, other):
         return pltpu.make_async_remote_copy(
@@ -99,21 +101,23 @@
         )
 
     last = rows - HALO
+
+    def edge(row):
+        return pl.ds(pl.multiple_of(row, HALO), HALO)
+
     halos = []
-    for side, other, src_row, dst_row in (
-        (0, partner, last * (1 - par), (rows + HALO) * par),
-        (1, cross, last * par, (rows + HALO) * (1 - par)),
-    ):
-        for which, src, dst in ((0, q_hbm, qb), (1, r_hbm, rb)):
-            halos.append(
-                remote(
-                    src.at[pl.ds(pl.multiple_of(src_row, HALO), HALO)],
-                    dst.at[pl.ds(pl.multiple_of(dst_row, HALO), HALO)],
-                    halo_send.at[side, which],
-                    halo_recv.at[side, which],
-                    other,
-                )
-            )
+    for which, src, dst in ((0, q_hbm, qb), (1, r_hbm, rb)):
+        ends = (
+            (src.at[edge(last * (1 - par))], dst.at[edge((rows + HALO) * par)], partner),
+            (src.at[edge(last * par)], passing.at[which], partner),
+            (passing.at[which], dst.at[edge((rows + HALO) * par)], far),
+        )
+        halos.append(
+            [
+                remote(*ends[kind][:2], halo_send.at[kind, which], halo_recv.at[kind, which], ends[kind][2])
+                for kind in range(3)
+            ]
+        )
 
     def columns(c):
         return pl.ds(pl.multiple_of(c * 128, 128), 128)
@@ -128,9 +132,9 @@
         src = kv.at[which, pl.ds(2 * rows, rows)] if src is None else src
         src = src.at[:, cols]
         if kind == 0:
-            args = src, dst.at[pl.ds(0, rows), cols], up
+            args = src, dst.at[place(4 * rows * (1 - par)), cols], near
         elif kind == 1:
-            args = src, dst.at[pl.ds(4 * rows, rows), cols], down
+            args = src, dst.at[place(4 * rows * par), cols], far
         elif kind == 2:
             args = src, dst.at[place(rows + 2 * rows * par), cols], partner
         else:
@@ -147,17 +151,25 @@
             args[2],
         )
 
-    for copy in halos:
-        copy.start()
-
-    for which in (0, 1):
-
-        def start_chunk(c, carry, which=which):
-            for kind in (0, 1, 2):
+    for kind in (1, 0):
+        for pair in halos:
+            pair[kind].start()
+
+    def begin(kinds, which):
+        def start_chunk(c, carry):
+            for kind in kinds:
                 send(c, kind, which).start()
             return carry
 
         lax.fori_loop(0, n_chunks, start_chunk, 0)
+
+    begin((0, 2), 0)
+    for pair in halos:
+        pair[1].wait_recv()
+        pair[2].start()
+    begin((1,), 0)
+    begin((0, 2), 1)
+    begin((1,), 1)
 
     for copy in small:
         copy.wait()
@@ -190,8 +202,9 @@
 
     for copy in own:
         copy.wait()
-    for copy in halos:
-        copy.wait_recv()
+    for pair in halos:
+        pair[0].wait_recv()
+        pair[2].wait_recv()
 
     tile = q_rows // TILES
     window = WINDOW
@@ -201,7 +214,7 @@
     hi = (1.0 - is_even).astype(jnp.bfloat16)
     ones = jnp.ones((window, 128), jnp.bfloat16)
 
-    mx[:, columns(0)] = jnp.zeros((q_rows, 128), jnp.float32)
+    mxs[1] = jnp.zeros((q_rows, 128), jnp.float32)
     half = taps_ref.shape[0] // 2
 
     def weigh(c):
@@ -225,7 +238,7 @@
             m = jnp.max(s, axis=1, keepdims=True)
             pb[c * TILES + t] = jnp.exp(s - m).astype(jnp.bfloat16)
 
-    def convolve(c):
+    def convolve(c, mx, cv):
         cols = columns(c)
         for r in range(0, rows, CONV_ROWS):
             some = pl.ds(r, CONV_ROWS)
@@ -234,7 +247,7 @@
             acc = jnp.zeros((CONV_ROWS, 128), jnp.float32)
             for j in range(2 * half + 1):
                 by = j - half
-                x = mx[pl.ds(r + HALO + by, CONV_ROWS), cols]
+                x = mx[pl.ds(r + HALO + by, CONV_ROWS), :]
                 if by < 0:
                     x = jnp.where(room_before >= float(-by), x, 0.0)
                 elif by > 0:
@@ -242,7 +255,7 @@
                 acc = acc + x * taps_ref[pl.ds(j, 1), cols]
             cv[some, cols] = acc
 
-    def mix(c):
+    def mix(c, mx):
         cols = columns(c)
         for t in range(TILES):
             mine = pl.ds(t * tile, tile)
@@ -252,34 +265,48 @@
             num = jnp.where(even, o[:tile, :128], o[tile:, :128])
             den = jnp.where(even, o[:tile, 128:], o[tile:, 128:])
             mixed = rb[mine, cols].astype(jnp.float32) + num / den
-            mx[mine, cols] = mixed.astype(jnp.bfloat16).astype(jnp.float32)
-
-    def step(i, carry):
-        @pl.when(i < 2 * n_chunks)
-        def _():
-            which, c = i // n_chunks, i % n_chunks
-            for kind in (0, 1):
-                send(c, kind, which).wait_recv()
-            send(c, 3, which).start()
-
-        @pl.when((i >= 1) & (i <= n_chunks))
-        def _():
-            for kind in (2, 3):
-                send(i - 1, kind, 0).wait_recv()
-            weigh(i - 1)
-
-        @pl.when(i > n_chunks)
-        def _():
-            c = i - 1 - n_chunks
-            for kind in (2, 3):
-                send(c, kind, 1).wait_recv()
-            convolve(lax.max(c - 1, 0))
-            mix(c)
-
+            mx[mine, :] = mixed.astype(jnp.bfloat16).astype(jnp.float32)
+
+    def take(i):
+        which, c = i // n_chunks, i % n_chunks
+        send(c, 0, which).wait_recv()
+        send(c, 3, which).start()
+
+    def ready(c, which):
+        for kind in (2, 3, 1):
+            send(c, kind, which).wait_recv()
+
+    take(0)
+
+    def weigh_step(c, carry):
+        take(c + 1)
+        ready(c, 0)
+        weigh(c)
         return carry
 
-    lax.fori_loop(0, 2 * n_chunks + 1, step, 0)
-    convolve(n_chunks - 1)
+    lax.fori_loop(0, n_chunks, weigh_step, 0)
+
+    def keep(c, a):
+        cols = columns(c)
+        mb[:, cols] = mxs[a, pl.ds(HALO, rows), :].astype(jnp.bfloat16)
+
+    def mix_step(j, carry):
+        for a in (0, 1):
+            c = 2 * j + a
+            prev = lax.max(c - 1, 0)
+            convolve(prev, mxs.at[1 - a], cv)
+
+            @pl.when(c + 1 < n_chunks)
+            def _():
+                take(n_chunks + c + 1)
+
+            ready(c, 1)
+            mix(c, mxs.at[a])
+            keep(c, a)
+        return carry
+
+    lax.fori_loop(0, n_chunks // 2, mix_step, 0)
+    convolve(n_chunks - 1, mxs.at[1], cv)
 
     for r in range(0, rows, NORM_ROWS):
         some = pl.ds(r, NORM_ROWS)
@@ -290,11 +317,12 @@
         normed = x * lax.rsqrt(var + 1e-05) * gain_ref[...] + shift_ref[...]
         gated = 0.5 * normed
         gated = gated + gated * jnp.tanh(gated)
-        result = mx[pl.ds(r + HALO, NORM_ROWS), :] + gated
+        result = mb[some, :].astype(jnp.float32) + gated
         out_ref[some, :] = result.astype(out_ref.dtype)
 
-    for copy in halos:
-        copy.wait_send()
+    for pair in halos:
+        for copy in pair:
+            copy.wait_send()
 
     def finish(c, carry):
         for kind in range(4):
@@ -332,6 +360,7 @@
             pltpu.VMEM(depth_kernel.shape, f32),
             pltpu.VMEM((1, width), f32),
             pltpu.VMEM((1, width), f32),
+            pltpu.VMEM((2, HALO, width), bf16),
             pltpu.VMEM((q_rows, width), bf16),
             pltpu.VMEM((q_rows, width), bf16),
             pltpu.VMEM((2, span, width), bf16),
@@ -341,12 +370,14 @@
             pltpu.VMEM((q_rows, 128), bf16),
             pltpu.VMEM((rows, 128), f32),
             pltpu.VMEM((rows, 128), f32),
-            pltpu.VMEM((q_rows, width), f32),
+            pltpu.VMEM((2, q_rows, 128), f32),
+            pltpu.VMEM((rows, 128), f32),
+            pltpu.VMEM((rows, width), bf16),
             pltpu.VMEM((rows, width), f32),
             pltpu.SemaphoreType.DMA((4,)),
             pltpu.SemaphoreType.DMA((4,)),
-            pltpu.SemaphoreType.DMA((2, 2)),
-            pltpu.SemaphoreType.DMA((2, 2)),
+            pltpu.SemaphoreType.DMA((3, 2)),
+            pltpu.SemaphoreType.DMA((3, 2)),
             pltpu.SemaphoreType.DMA((4, n_chunks, 2)),
             pltpu.SemaphoreType.DMA((4, n_chunks, 2)),
         ],

time: 49.6 us -> 46.4 us (0.935)
  Pallas kernels: 48.6 us -> 45.4 us
    pallas_call x1, Pallas kernels: 48.6 us -> 45.4 us  [local(): pl.pallas_call(functools.partial(block_kernel, n), out_shape=jax.ShapeDty...]
where the time goes in v1:
time: 46.4 us; the launch traced here: 46.3 us
  Pallas kernels  45.4 us (98%)
  local copies, waits for them, and re-layouts  0.84 us (2%)
    pallas_call x1, Pallas kernels, local(): pl.pallas_call(functools.partial(block_kernel, n), out_shape=jax.ShapeDty...  45.4 us

profile of v1, /device:TPU:1, one launch (start us, length us, event | category | flops | bytes accessed | tf_op | source)
XLA Modules:
  0.0 46.3 jit_solution(17299489458484904289)
XLA Ops:
  0.0 45.4 %conformer_block.1 = bf16[320,1024]{1,0:T(8,128)(2,1)S(1)} custom-call(s32[1,64]{1,0:T(1,128)} %bitcast.5, f32[31,1024]{1,0:T(8,128)} %taps_hbm.1, f32[1,1024]{1,0:T(1,128)} %bitcast.3, f32[1,1024]{1,0:T(1,128)} %bitcast.4, bf16[320,1024]{1,0:T(8,128)(2,1)} %q_hbm.1, bf16[320,1024]{1,0:T(8,128)(2,1)} %k_hbm.1, bf16[320,1024]{1,0:T(8,128)(2,1)} %v_hbm.1, ...), custom_call_target="tpu_custom_call" | custom-call | tf_op jit(solution)/shard_map/conformer_block/pallas_call | solution.py:353
  45.4 0.8 %copy.10 = bf16[320,1024]{1,0:T(8,128)(2,1)} copy(bf16[320,1024]{1,0:T(8,128)(2,1)S(1)} %conformer_block.1) | data formatting | bytes 1310720

commit v2 on v1

--- a/solution.py
+++ b/solution.py
@@ -13,6 +13,7 @@
 CONV_ROWS = 64
 NORM_ROWS = 32
 WINDOW = 1536
+AHEAD = 1
 APART = -4096.0
 
 
@@ -41,8 +42,9 @@
     qf,
     after,
     before,
+    keeps,
+    lag,
     mxs,
-    cvs,
     mb,
     cv,
     small_sem,
@@ -63,6 +65,10 @@
     near = (me + n - 2 + 4 * par) % n
     far = (me + n + 2 - 4 * par) % n
 
+    barrier = pltpu.get_barrier_semaphore()
+    for other in (partner, near, far):
+        pl.semaphore_signal(barrier, inc=1, device_id={"seq": other}, device_id_type=MESH)
+
     small = [
         pltpu.make_async_copy(src, dst, small_sem.at[i])
         for i, (src, dst) in enumerate(
@@ -85,9 +91,6 @@
     for copy in own:
         copy.start()
 
-    barrier = pltpu.get_barrier_semaphore()
-    for other in (partner, near, far):
-        pl.semaphore_signal(barrier, inc=1, device_id={"seq": other}, device_id_type=MESH)
     pl.semaphore_wait(barrier, 3)
 
     def remote(src, dst, ssem, rsem, other):
@@ -151,23 +154,26 @@
             args[2],
         )
 
-    for kind in (1, 0):
-        for pair in halos:
-            pair[kind].start()
-
-    def begin(kinds, which):
+    def begin(kinds, which, first=0):
         def start_chunk(c, carry):
             for kind in kinds:
                 send(c, kind, which).start()
             return carry
 
-        lax.fori_loop(0, n_chunks, start_chunk, 0)
-
-    begin((0, 2), 0)
+        lax.fori_loop(first, n_chunks, start_chunk, 0)
+
+    for c in range(AHEAD):
+        send(c, 0, 0).start()
+        send(c, 1, 0).start()
+    for kind in (1, 0):
+        for pair in halos:
+            pair[kind].start()
+    begin((0,), 0, AHEAD)
+    begin((2,), 0)
     for pair in halos:
         pair[1].wait_recv()
         pair[2].start()
-    begin((1,), 0)
+    begin((1,), 0, AHEAD)
     begin((0, 2), 1)
     begin((1,), 1)
 
@@ -197,8 +203,17 @@
     pos, inside = member(base, rows)
     first = jnp.sum(jnp.where(inside, starts, 0.0), axis=1, keepdims=True)
     final = jnp.sum(jnp.where(inside, ends, 0.0), axis=1, keepdims=True)
-    before[...] = pos - first
-    after[...] = final - 1.0 - pos
+    shifted = rows + 8
+    half = taps_ref.shape[0] // 2
+    for room, value in ((before, pos - first), (after, final - 1.0 - pos)):
+        room[pl.ds(0, 8), :] = jnp.full((8, 128), -1.0, jnp.float32)
+        room[pl.ds(shifted, 8), :] = jnp.full((8, 128), -1.0, jnp.float32)
+        room[pl.ds(8, rows), :] = jnp.broadcast_to(value, (rows, 128))
+    for j in range(2 * half + 1):
+        if j != half:
+            room = before if j < half else after
+            near_rows = room[pl.ds(8 - (j + 1) % 8, shifted), :]
+            keeps[j] = jnp.where(near_rows >= float(abs(j - half)), 1.0, 0.0)
 
     for copy in own:
         copy.wait()
@@ -215,8 +230,6 @@
     ones = jnp.ones((window, 128), jnp.bfloat16)
 
     mxs[1] = jnp.zeros((q_rows, 128), jnp.float32)
-    half = taps_ref.shape[0] // 2
-
     def weigh(c):
         cols = columns(c)
         for t in range(TILES):
@@ -240,20 +253,23 @@
 
     def convolve(c, mx, cv):
         cols = columns(c)
-        for r in range(0, rows, CONV_ROWS):
-            some = pl.ds(r, CONV_ROWS)
-            room_before = before[some, :]
-            room_after = after[some, :]
-            acc = jnp.zeros((CONV_ROWS, 128), jnp.float32)
-            for j in range(2 * half + 1):
-                by = j - half
-                x = mx[pl.ds(r + HALO + by, CONV_ROWS), :]
-                if by < 0:
-                    x = jnp.where(room_before >= float(-by), x, 0.0)
-                elif by > 0:
-                    x = jnp.where(room_after >= float(by), x, 0.0)
-                acc = acc + x * taps_ref[pl.ds(j, 1), cols]
-            cv[some, cols] = acc
+        for y in range(0, shifted, CONV_ROWS):
+            count = min(CONV_ROWS, shifted - y)
+            for r in range(8):
+                acc = None
+                for j in range(taps_ref.shape[0]):
+                    if (j + 1) % 8 == r:
+                        x = mx[pl.ds(y + j + 1 - r, count), :]
+                        if j != half:
+                            x = x * keeps[j, pl.ds(y, count), :]
+                        x = x * taps_ref[pl.ds(j, 1), cols]
+                        acc = x if acc is None else acc + x
+                lag[r, pl.ds(y, count), :] = acc
+        for t in range(0, rows, CONV_ROWS):
+            acc = lag[0, pl.ds(t, CONV_ROWS), :]
+            for r in range(1, 8):
+                acc = acc + lag[r, pl.ds(t + r, CONV_ROWS), :]
+            cv[pl.ds(t, CONV_ROWS), cols] = acc
 
     def mix(c, mx):
         cols = columns(c)
@@ -286,6 +302,10 @@
 
     lax.fori_loop(0, n_chunks, weigh_step, 0)
 
+    for pair in halos:
+        for copy in pair:
+            copy.wait_send()
+
     def keep(c, a):
         cols = columns(c)
         mb[:, cols] = mxs[a, pl.ds(HALO, rows), :].astype(jnp.bfloat16)
@@ -303,6 +323,14 @@
             ready(c, 1)
             mix(c, mxs.at[a])
             keep(c, a)
+            for kind in range(4):
+                send(c, kind, 0).wait_send()
+
+            @pl.when(c > 0)
+            def _():
+                for kind in range(4):
+                    send(c - 1, kind, 1).wait_send()
+
         return carry
 
     lax.fori_loop(0, n_chunks // 2, mix_step, 0)
@@ -320,17 +348,8 @@
         result = mb[some, :].astype(jnp.float32) + gated
         out_ref[some, :] = result.astype(out_ref.dtype)
 
-    for pair in halos:
-        for copy in pair:
-            copy.wait_send()
-
-    def finish(c, carry):
-        for kind in range(4):
-            for which in (0, 1):
-                send(c, kind, which).wait_send()
-        return carry
-
-    lax.fori_loop(0, n_chunks, finish, 0)
+    for kind in range(4):
+        send(n_chunks - 1, kind, 1).wait_send()
 
 
 def local(
@@ -368,10 +387,11 @@
             pltpu.VMEM((1, 128), f32),
             pltpu.VMEM((span, 128), bf16),
             pltpu.VMEM((q_rows, 128), bf16),
-            pltpu.VMEM((rows, 128), f32),
-            pltpu.VMEM((rows, 128), f32),
+            pltpu.VMEM((rows + 16, 128), f32),
+            pltpu.VMEM((rows + 16, 128), f32),
+            pltpu.VMEM((depth_kernel.shape[0], rows + 8, 128), f32),
+            pltpu.VMEM((8, rows + 8, 128), f32),
             pltpu.VMEM((2, q_rows, 128), f32),
-            pltpu.VMEM((rows, 128), f32),
             pltpu.VMEM((rows, width), bf16),
             pltpu.VMEM((rows, width), f32),
             pltpu.SemaphoreType.DMA((4,)),

time: 46.4 us -> 45.2 us (0.974)
  Pallas kernels: 45.4 us -> 44.2 us
    pallas_call x1, Pallas kernels: 45.4 us -> 44.2 us  [local(): pl.pallas_call(functools.partial(block_kernel, n), out_shape=jax.ShapeDty...]
where the time goes in v2:
time: 45.2 us; the launch traced here: 45.1 us
  Pallas kernels  44.2 us (98%)
  local copies, waits for them, and re-layouts  0.84 us (2%)
    pallas_call x1, Pallas kernels, local(): pl.pallas_call(functools.partial(block_kernel, n), out_shape=jax.ShapeDty...  44.2 us

profile of v2, /device:TPU:1, one launch (start us, length us, event | category | flops | bytes accessed | tf_op | source)
XLA Modules:
  0.0 45.1 jit_solution(3444710540906977895)
XLA Ops:
  0.0 44.2 %conformer_block.1 = bf16[320,1024]{1,0:T(8,128)(2,1)S(1)} custom-call(s32[1,64]{1,0:T(1,128)} %bitcast.5, f32[31,1024]{1,0:T(8,128)} %taps_hbm.1, f32[1,1024]{1,0:T(1,128)} %bitcast.3, f32[1,1024]{1,0:T(1,128)} %bitcast.4, bf16[320,1024]{1,0:T(8,128)(2,1)} %q_hbm.1, bf16[320,1024]{1,0:T(8,128)(2,1)} %k_hbm.1, bf16[320,1024]{1,0:T(8,128)(2,1)} %v_hbm.1, ...), custom_call_target="tpu_custom_call" | custom-call | tf_op jit(solution)/shard_map/conformer_block/pallas_call | solution.py:372
  44.2 0.8 %copy.10 = bf16[320,1024]{1,0:T(8,128)(2,1)} copy(bf16[320,1024]{1,0:T(8,128)(2,1)S(1)} %conformer_block.1) | data formatting | bytes 1310720

commit v3 on v2

--- a/solution.py
+++ b/solution.py
@@ -11,9 +11,9 @@
 HALO = 16
 TILES = 2
 CONV_ROWS = 64
-NORM_ROWS = 32
+NORM_ROWS = 16
 WINDOW = 1536
-AHEAD = 1
+AHEAD = 2
 APART = -4096.0
 
 
@@ -314,7 +314,13 @@
         for a in (0, 1):
             c = 2 * j + a
             prev = lax.max(c - 1, 0)
-            convolve(prev, mxs.at[1 - a], cv)
+            if a:
+                convolve(prev, mxs.at[0], cv)
+            else:
+
+                @pl.when(c > 0)
+                def _():
+                    convolve(prev, mxs.at[1], cv)
 
             @pl.when(c + 1 < n_chunks)
             def _():

time: 45.2 us -> 45.1 us (level)
  no operation moved by 1% of the time
where the time goes in v3:
time: 45.1 us; the launch traced here: 45 us
  Pallas kernels  44.2 us (98%)
  local copies, waits for them, and re-layouts  0.84 us (2%)
    pallas_call x1, Pallas kernels, local(): pl.pallas_call(functools.partial(block_kernel, n), out_shape=jax.ShapeDty...  44.2 us

profile of v3, /device:TPU:1, one launch (start us, length us, event | category | flops | bytes accessed | tf_op | source)
XLA Modules:
  0.0 45.0 jit_solution(6419568025560851712)
XLA Ops:
  0.0 44.2 %conformer_block.1 = bf16[320,1024]{1,0:T(8,128)(2,1)S(1)} custom-call(s32[1,64]{1,0:T(1,128)} %bitcast.5, f32[31,1024]{1,0:T(8,128)} %taps_hbm.1, f32[1,1024]{1,0:T(1,128)} %bitcast.3, f32[1,1024]{1,0:T(1,128)} %bitcast.4, bf16[320,1024]{1,0:T(8,128)(2,1)} %q_hbm.1, bf16[320,1024]{1,0:T(8,128)(2,1)} %k_hbm.1, bf16[320,1024]{1,0:T(8,128)(2,1)} %v_hbm.1, ...), custom_call_target="tpu_custom_call" | custom-call | tf_op jit(solution)/shard_map/conformer_block/pallas_call | solution.py:378
  44.2 0.8 %copy.10 = bf16[320,1024]{1,0:T(8,128)(2,1)} copy(bf16[320,1024]{1,0:T(8,128)(2,1)S(1)} %conformer_block.1) | data formatting | bytes 1310720
